TPU v7x, 256 devices: a whole 4x4x8 slice. The times are simulated.
256 devices in a mesh: dp: 4 (over x), expert: 64 (over z, y, core).
Axes of the slice: x: 4, y: 4, z: 8, core: 2. Of those that a mesh axis runs over, the one named last changes fastest.
Arguments:
- cell_table: bfloat16 [524288, 256], P(('dp', 'expert')), may hold values from -6 to 6
- sample_index: int32 [262144], P(('dp', 'expert')), may hold values from 0 to 2047
- region: int32 [262144, 1], P(('dp', 'expert')), may hold values from 0 to 63; in each aligned block of 1024 rows (0 to 1023, 1024 to 2047, ...) at most 32 rows name the same one
- targets: bfloat16 [262144, 256], P(('dp', 'expert')), may hold values from -6 to 6
- trunk_weight: bfloat16 [256, 256], replicated, may hold values from -0.375 to 0.375
- expert_params: float32 [64, 2, 256, 2048], P('expert', None, None, 'dp'), may hold values from -0.375 to 0.375
- first_moment: float32 [64, 2, 256, 2048], P('expert', None, None, 'dp'), may hold values from -4 to 4
- second_moment: float32 [64, 2, 256, 2048], P('expert', None, None, 'dp'), may hold values from 0.05 to 1
Outputs:
- trunk_grad: float32 [256, 256], replicated
- row_loss: float32 [262144], P(('dp', 'expert'))
- new_params: float32 [64, 2, 256, 2048], P('expert', None, None, 'dp')
- new_first: float32 [64, 2, 256, 2048], P('expert', None, None, 'dp')
- new_second: float32 [64, 2, 256, 2048], P('expert', None, None, 'dp')
Inputs may be any that keep to these rules, and one draw needn't show every extreme that they name: In the 1024 rows of one device no region is named more than 32 times; some region exactly 32 times. `sample_index`: indexes the rows of the same device's block of cell_table.
All inputs are finite; a program needn't handle non-finite values.
Results may differ from a plain program's by a relative error of at most 0.0044.
Values may be sent and summed in bfloat16 or wider, within the bound.
A program may use at most 128 MiB of HBM per device.

v0:
```python
import jax
import jax.numpy as jnp
from jax import lax
from jax.sharding import PartitionSpec as P

loss_scale = 1.0 / 32.0
beta_one = 0.9
beta_two = 0.999
learn_rate = 0.05
adam_eps = 1e-08
adam_step = 10


def silu_slope(values):
    sigma = jax.nn.sigmoid(values)
    return sigma * (1.0 + values * (1.0 - sigma))


def expert_forward(arrived, w_up, w_down):
    up_pre = jnp.dot(arrived, w_up, preferred_element_type=jnp.float32)
    hidden = jax.nn.silu(up_pre).astype(jnp.bfloat16)
    predicted = lax.dot_general(
        hidden, w_down, (((1,), (1,)), ((), ())), preferred_element_type=jnp.float32
    )
    return (up_pre, hidden, predicted)


def expert_backward(arrived, up_pre, hidden, scaled_error, w_up, w_down):
    grad_down = lax.dot_general(
        scaled_error, hidden, (((0,), (0,)), ((), ())), preferred_element_type=jnp.float32
    )
    hidden_grad = jnp.dot(scaled_error, w_down, preferred_element_type=jnp.float32)
    pre_grad = (hidden_grad * silu_slope(up_pre)).astype(jnp.bfloat16)
    grad_up = lax.dot_general(
        arrived, pre_grad, (((0,), (0,)), ((), ())), preferred_element_type=jnp.float32
    )
    input_grad = lax.dot_general(
        pre_grad, w_up, (((1,), (1,)), ((), ())), preferred_element_type=jnp.float32
    ).astype(jnp.bfloat16)
    return (grad_up, grad_down, input_grad)


def error_terms(predicted, target):
    errors = predicted - target.astype(jnp.float32)
    losses = jnp.sum(errors * errors, axis=1) * (0.5 * loss_scale)
    return (losses, (errors * loss_scale).astype(jnp.bfloat16))


def adam_update(params, first, second, grads):
    first_new = beta_one * first + (1.0 - beta_one) * grads
    second_new = beta_two * second + (1.0 - beta_two) * grads * grads
    first_hat = first_new / (1.0 - beta_one**adam_step)
    second_hat = second_new / (1.0 - beta_two**adam_step)
    return (
        params - learn_rate * first_hat / (jnp.sqrt(second_hat) + adam_eps),
        first_new,
        second_new,
    )


def on_device(
    cell_table,
    sample_index,
    region,
    targets,
    trunk_weight,
    expert_params,
    first_moment,
    second_moment,
):
    rows = sample_index.shape[0]
    width = cell_table.shape[1]
    experts = lax.axis_size("expert")
    capacity = 2 * rows // experts
    features = jnp.take(cell_table, sample_index, axis=0)
    trunk_pre = jnp.dot(features, trunk_weight, preferred_element_type=jnp.float32)
    trunk_out = (features.astype(jnp.float32) + jax.nn.silu(trunk_pre)).astype(jnp.bfloat16)
    routed = region[:, 0]
    onehot = (routed[:, None] == jnp.arange(experts, dtype=jnp.int32)[None, :]).astype(jnp.int32)
    slots = jnp.sum(jnp.cumsum(onehot, axis=0) * onehot, axis=1) - 1
    places = routed * capacity + slots

    def pack(values):
        empty = jnp.zeros((experts * capacity,) + values.shape[1:], values.dtype)
        return empty.at[places].set(values).reshape((experts, capacity) + values.shape[1:])

    gathered = lax.all_gather(expert_params.astype(jnp.bfloat16), "dp", axis=3, tiled=True)
    w_up = gathered[0, 0]
    w_down = gathered[0, 1]
    arrived = lax.all_to_all(
        pack(trunk_out), "expert", split_axis=0, concat_axis=0, tiled=True
    ).reshape(-1, width)
    up_pre, hidden, predicted = expert_forward(arrived, w_up, w_down)
    returned = lax.all_to_all(
        predicted.reshape(experts, capacity, width),
        "expert",
        split_axis=0,
        concat_axis=0,
        tiled=True,
    )
    row_loss, row_error = error_terms(returned.reshape(-1, width)[places], targets)
    error_there = lax.all_to_all(
        pack(row_error), "expert", split_axis=0, concat_axis=0, tiled=True
    ).reshape(-1, width)
    grad_up, grad_down, input_grad = expert_backward(
        arrived, up_pre, hidden, error_there, w_up, w_down
    )
    back_grad = lax.all_to_all(
        input_grad.reshape(experts, capacity, width),
        "expert",
        split_axis=0,
        concat_axis=0,
        tiled=True,
    )
    row_grad = back_grad.reshape(-1, width)[places]
    trunk_slope = (row_grad.astype(jnp.float32) * silu_slope(trunk_pre)).astype(jnp.bfloat16)
    trunk_local = lax.dot_general(
        features, trunk_slope, (((0,), (0,)), ((), ())), preferred_element_type=jnp.float32
    )
    trunk_grad = lax.psum(trunk_local, ("dp", "expert"))
    grads = jnp.stack([grad_up, grad_down])[None]
    grad_shard = lax.psum_scatter(grads, "dp", scatter_dimension=3, tiled=True)
    new_params, new_first, new_second = adam_update(
        expert_params, first_moment, second_moment, grad_shard
    )
    return (trunk_grad, row_loss, new_params, new_first, new_second)


def solution(mesh):
    placed = (
        P(("dp", "expert"), None),
        P(("dp", "expert")),
        P(("dp", "expert"), None),
        P(("dp", "expert"), None),
        P(),
        P("expert", None, None, "dp"),
        P("expert", None, None, "dp"),
        P("expert", None, None, "dp"),
    )
    return jax.shard_map(
        on_device,
        mesh=mesh,
        in_specs=placed,
        out_specs=(
            P(),
            P(("dp", "expert")),
            P("expert", None, None, "dp"),
            P("expert", None, None, "dp"),
            P("expert", None, None, "dp"),
        ),
        check_vma=False,
    )
```

profile of v0, /device:TPU:2, one launch (start us, length us, event | category | flops | bytes accessed | tf_op | source)
XLA Modules:
  0.0 533.0 jit_solution(5352181415112622577)
XLA Ops:
  7.2 0.0 copy-start
  7.2 0.0 copy-start.11
  7.2 0.0 copy-start.12
  7.2 0.0 all-gather.2.cloned.1.call-start
  7.3 2.2 convert_element_type.38
  9.4 0.0 all-gather.2.cloned.1.call-update
  9.5 0.7 fusion.15
  10.2 18.0 %reduce-window.6 = s32[64,8,128]{2,1,0:T(8,128)S(1)} reduce-window(s32[64,8,128]{2,1,0:T(8,128)S(1)} %fusion.15, s32[]{:T(128)} %constant.18.clone.1), window={size=1x1x128 pad=0_0x0_0x127_0}, to_apply=%region_0.1 | reduce-window | flops 8323072 | bytes 524292 | tf_op jit(solution)/shard_map/reduce-window
  28.2 0.1 slice.22
  28.3 0.1 copy.13
  28.5 0.1 copy.14
  28.6 0.1 broadcast_add_fusion
  28.7 0.7 fusion.16
  29.4 3.9 gather_fusion
  33.4 0.1 fusion.14
  33.5 0.4 fusion.18
  33.9 0.0 copy-start.8
  33.9 6.0 %scatter_custom_fusion = bf16[2048,256]{1,0:T(8,128)(2,1)S(1)} fusion(s32[1024]{0:T(1024)S(1)} %bitcast.70, bf16[]{:T(256)} %constant.22.clone.1, f32[1024,256]{1,0:T(8,128)S(1)} %fusion.18, f32[]{:T(128)} %constant.15.clone.1, bf16[1024,256]{1,0:T(8,128)(2,1)S(1)} %gather_fusion, pred[1024]{0:T(1024)(128)(4,1)S(1)} %compare_and_fusion), kind=kCustom, calls=%fused_computation.32 | custom fusion | flops 2097152 | bytes 2622470 | tf_op jit(solution)/shard_map/scatter | solution.py:85
  39.9 40.8 %all_to_all.20 = bf16[64,32,256]{2,1,0:T(8,128)(2,1)S(1)} all-to-all(bf16[64,32,256]{2,1,0:T(8,128)(2,1)S(1)} %bitcast.64), channel_id=1, replica_groups=mesh['dp'=4,'expert'=64] {'expert'}, dimensions={0} | all-to-all | bytes 2097152 | tf_op jit(solution)/shard_map/all_to_all | solution.py:90
  80.7 9.8 %multiply_convert_fusion.1 = (bf16[2048,2048]{1,0:T(8,128)(2,1)S(1)}, f32[2048,2048]{1,0:T(8,128)}) fusion(bf16[2048,256]{1,0:T(8,128)(2,1)S(1)} %bitcast.59, bf16[1,2,256,2048]{3,2,1,0:T(8,128)(2,1)} %all-gather.2.cloned.1.call-done), kind=kOutput, calls=%fused_computation.6 | convolution fusion | flops 2168455168 | bytes 27262976 | tf_op jit(solution)/shard_map/dot_general | solution.py:20
  90.5 3.2 copy-done.2
  93.8 3.8 fusion.1
  97.6 5.6 %all-to-all-start.1 = ((f32[64,32,256]{2,1,0:T(8,128)}), f32[64,32,256]{2,1,0:T(8,128)S(1)}, u32[]{:S(2)}, u32[]{:S(2)}) async-start(f32[64,32,256]{2,1,0:T(8,128)} %fusion.1), calls=%async_computation.1 | async-start | bytes 4194304 | tf_op jit(solution)/shard_map/all_to_all | solution.py:94
  103.1 0.2 reduce-scatter.2.cloned.1.call-start
  103.4 51.1 %all-to-all-done.1 = f32[64,32,256]{2,1,0:T(8,128)S(1)} async-done(((f32[64,32,256]{2,1,0:T(8,128)}), f32[64,32,256]{2,1,0:T(8,128)S(1)}, u32[]{:S(2)}, u32[]{:S(2)}) %all-to-all-start.1) | async-done | bytes 2097184 | tf_op jit(solution)/shard_map/all_to_all | solution.py:94
  154.5 3.5 gather_fusion.1
  157.9 5.7 %scatter_custom_fusion.1 = bf16[2048,256]{1,0:T(8,128)(2,1)S(1)} fusion(s32[1024]{0:T(1024)S(1)} %bitcast.72, f32[1024,256]{1,0:T(8,128)S(1)} %gather_fusion.1, bf16[1024,256]{1,0:T(8,128)(2,1)} %param.11, f32[]{:T(128)} %constant.16.clone.1, bf16[]{:T(256)} %constant.22.clone.1), kind=kCustom, calls=%fused_computation.29 | custom fusion | flops 1048576 | bytes 2621446 | tf_op jit(solution)/shard_map/scatter | solution.py:85
  163.7 34.0 %all_to_all.21 = bf16[64,32,256]{2,1,0:T(8,128)(2,1)S(1)} all-to-all(bf16[64,32,256]{2,1,0:T(8,128)(2,1)S(1)} %bitcast.63), channel_id=1, replica_groups=mesh['dp'=4,'expert'=64] {'expert'}, dimensions={0} | all-to-all | bytes 2097152 | tf_op jit(solution)/shard_map/all_to_all | solution.py:102
  197.7 5.9 %convolution_bitcast_fusion = f32[1,256,2048]{2,1,0:T(8,128)S(1)} fusion(bf16[2048,256]{1,0:T(8,128)(2,1)S(1)} %bitcast.61, bf16[2048,2048]{1,0:T(8,128)(2,1)} %copy-done.2), kind=kOutput, calls=%fused_computation.9 | convolution fusion | flops 2147483648 | bytes 11534336 | tf_op jit(solution)/shard_map/dot_general | solution.py:29
  203.6 10.4 %multiply_convert_fusion = bf16[2048,2048]{1,0:T(8,128)(2,1)S(1)} fusion(f32[2048,2048]{1,0:T(8,128)} %get-tuple-element.9, bf16[2048,256]{1,0:T(8,128)(2,1)S(1)} %bitcast.62, bf16[1,2,256,2048]{3,2,1,0:T(8,128)(2,1)S(1)} %copy-done.14), kind=kOutput, calls=%fused_computation.5 | convolution fusion | flops 2185232384 | bytes 27262976 | tf_op jit(solution)/shard_map/dot_general | solution.py:32
  214.0 3.2 copy-done.3
  217.2 2.3 convolution_bitcast_fusion.1
  219.6 2.2 maximum_bitcast_fusion
  221.8 0.0 reduce-scatter.2.cloned.1.call-update
  221.8 0.0 copy-start.9
  221.8 7.0 %convolution_convert_fusion = bf16[2048,256]{1,0:T(8,128)(2,1)} fusion(bf16[2048,2048]{1,0:T(8,128)(2,1)} %copy-done.3, bf16[1,2,256,2048]{3,2,1,0:T(8,128)(2,1)} %all-gather.2.cloned.1.call-done), kind=kOutput, calls=%fused_computation.11 | convolution fusion | flops 2148007936 | bytes 10485760 | tf_op jit(solution)/shard_map/dot_general | solution.py:37
  228.9 5.7 %all-to-all-start.3 = ((bf16[64,32,256]{2,1,0:T(8,128)(2,1)}), bf16[64,32,256]{2,1,0:T(8,128)(2,1)S(1)}, u32[]{:S(2)}, u32[]{:S(2)}) async-start(bf16[64,32,256]{2,1,0:T(8,128)(2,1)} %bitcast.65), calls=%async_computation.3 | async-start | bytes 2097152 | tf_op jit(solution)/shard_map/all_to_all | solution.py:108
  234.6 0.0 all-reduce.2.cloned.1.call-start
  234.6 0.2 multiply_reduce_fusion
  234.9 0.6 broadcast_multiply_fusion
  235.5 28.0 %all-to-all-done.3 = bf16[64,32,256]{2,1,0:T(8,128)(2,1)S(1)} async-done(((bf16[64,32,256]{2,1,0:T(8,128)(2,1)}), bf16[64,32,256]{2,1,0:T(8,128)(2,1)S(1)}, u32[]{:S(2)}, u32[]{:S(2)}) %all-to-all-start.3) | async-done | bytes 1048608 | tf_op jit(solution)/shard_map/all_to_all | solution.py:108
  263.5 3.9 gather_fusion.2
  267.4 2.7 fusion.12
  270.1 0.0 all-reduce.2.cloned.1.call-update
  270.1 0.0 reduce-scatter.2.cloned.1.call-done
  270.2 4.3 divide_subtract_fusion
  274.5 250.3 %all-reduce.2.cloned.1.call-done = f32[256,256]{1,0:T(8,128)} async-done(((f32[256,256]{1,0:T(8,128)}), f32[256,256]{1,0:T(8,128)}) %all-reduce.2.cloned.1.call-update) | async-done | bytes 262160 | tf_op jit(solution)/shard_map/psum | solution.py:120
  524.8 1.7 copy.18
  (30 shorter events, 0.1 us)
Async XLA Ops:
  7.2 22.3 %copy-start = (bf16[2048,256]{1,0:T(8,128)(2,1)S(1)}, bf16[2048,256]{1,0:T(8,128)(2,1)}, u32[]{:S(2)}) copy-start(bf16[2048,256]{1,0:T(8,128)(2,1)} %param.8) | copy-start | bytes 3145732
  7.2 26.2 %copy-start.11 = (s32[1024,1]{0,1:T(1,128)S(1)}, s32[1024,1]{0,1:T(1,128)}, u32[]{:S(2)}) copy-start(s32[1024,1]{0,1:T(1,128)} %param.10) | copy-start | bytes 12292
  7.2 26.3 %copy-start.12 = (s32[1024]{0:T(1024)S(1)}, s32[1024]{0:T(1024)}, u32[]{:S(2)}) copy-start(s32[1024]{0:T(1024)} %param.9) | copy-start | bytes 12292
  7.2 26.3 %copy-start.10 = (bf16[256,256]{1,0:T(8,128)(2,1)S(1)}, bf16[256,256]{1,0:T(8,128)(2,1)}, u32[]{:S(2)}) copy-start(bf16[256,256]{1,0:T(8,128)(2,1)} %param.12) | copy-start | bytes 393220
  7.2 73.5 %all-gather.2.cloned.1.call-start = ((), (), s32[]{:S(2)}) async-start(), calls=%async_computation.5 | async-start | bytes 2621440 | tf_op jit(solution)/shard_map/all_gather | solution.py:87
  33.4 57.2 %copy-start.6 = (bf16[1024,256]{1,0:T(8,128)(2,1)}, bf16[1024,256]{1,0:T(8,128)(2,1)S(1)}, u32[]{:S(2)}) copy-start(bf16[1024,256]{1,0:T(8,128)(2,1)S(1)} %gather_fusion) | copy-start | bytes 1572868
  33.9 6.0 %copy-start.8 = (f32[1024,256]{1,0:T(8,128)}, f32[1024,256]{1,0:T(8,128)S(1)}, u32[]{:S(2)}) copy-start(f32[1024,256]{1,0:T(8,128)S(1)} %fusion.18) | copy-start | bytes 3145732
  80.7 9.8 %copy-start.4 = (bf16[64,32,256]{2,1,0:T(8,128)(2,1)}, bf16[64,32,256]{2,1,0:T(8,128)(2,1)S(1)}, u32[]{:S(2)}) copy-start(bf16[64,32,256]{2,1,0:T(8,128)(2,1)S(1)} %all_to_all.20) | copy-start | bytes 3145732
  80.7 13.0 %copy-start.13 = (bf16[1,2,256,2048]{3,2,1,0:T(8,128)(2,1)S(1)}, bf16[1,2,256,2048]{3,2,1,0:T(8,128)(2,1)}, u32[]{:S(2)}) copy-start(bf16[1,2,256,2048]{3,2,1,0:T(8,128)(2,1)} %all-gather.2.cloned.1.call-done) | copy-start | bytes 6291460
  90.5 3.2 copy-start.2
  97.6 56.9 %all-to-all-start.1 = ((f32[64,32,256]{2,1,0:T(8,128)}), f32[64,32,256]{2,1,0:T(8,128)S(1)}, u32[]{:S(2)}, u32[]{:S(2)}) async-start(f32[64,32,256]{2,1,0:T(8,128)} %fusion.1), calls=%async_computation.1 | async-start | bytes 4194304 | tf_op jit(solution)/shard_map/all_to_all | solution.py:94
  103.1 167.0 %reduce-scatter.2.cloned.1.call-start = ((), (), s32[]{:S(2)}) async-start(), calls=%async_computation.7 | async-start | bytes 5242880 | tf_op jit(solution)/shard_map/reduce_scatter | solution.py:122
  197.7 5.9 %copy-start.14 = (bf16[1,2,256,2048]{3,2,1,0:T(8,128)(2,1)S(1)}, bf16[1,2,256,2048]{3,2,1,0:T(8,128)(2,1)}, u32[]{:S(2)}) copy-start(bf16[1,2,256,2048]{3,2,1,0:T(8,128)(2,1)} %all-gather.2.cloned.1.call-done) | copy-start | bytes 6291460
  203.6 13.6 %copy-start.5 = (bf16[64,32,256]{2,1,0:T(8,128)(2,1)S(1)}, bf16[64,32,256]{2,1,0:T(8,128)(2,1)}, u32[]{:S(2)}) copy-start(bf16[64,32,256]{2,1,0:T(8,128)(2,1)} %copy-done.4) | copy-start | bytes 3145732
  214.0 3.2 copy-start.3
  221.8 12.8 %copy-start.9 = (bf16[1024,256]{1,0:T(8,128)(2,1)S(1)}, bf16[1024,256]{1,0:T(8,128)(2,1)}, u32[]{:S(2)}) copy-start(bf16[1024,256]{1,0:T(8,128)(2,1)} %param.11) | copy-start | bytes 1572868
  228.9 38.5 %copy-start.7 = (bf16[1024,256]{1,0:T(8,128)(2,1)S(1)}, bf16[1024,256]{1,0:T(8,128)(2,1)}, u32[]{:S(2)}) copy-start(bf16[1024,256]{1,0:T(8,128)(2,1)} %copy-done.6) | copy-start | bytes 1572868
  228.9 34.6 %all-to-all-start.3 = ((bf16[64,32,256]{2,1,0:T(8,128)(2,1)}), bf16[64,32,256]{2,1,0:T(8,128)(2,1)S(1)}, u32[]{:S(2)}, u32[]{:S(2)}) async-start(bf16[64,32,256]{2,1,0:T(8,128)(2,1)} %bitcast.65), calls=%async_computation.3 | async-start | bytes 2097152 | tf_op jit(solution)/shard_map/all_to_all | solution.py:108
  234.6 290.2 %all-reduce.2.cloned.1.call-start = ((), (), s32[]{:S(2)}) async-start(), calls=%async_computation.6 | async-start | bytes 524288 | tf_op jit(solution)/shard_map/psum | solution.py:120
  263.5 263.0 %copy-start.1 = (bf16[2048,256]{1,0:T(8,128)(2,1)S(1)}, bf16[2048,256]{1,0:T(8,128)(2,1)}, u32[]{:S(2)}) copy-start(bf16[2048,256]{1,0:T(8,128)(2,1)} %param.8) | copy-start | bytes 3145732
Sparse Core Ops, SparseCore 0:
  10.4 35.3 all-gather.1
  222.0 44.4 reduce-scatter.1
  273.4 251.2 all-reduce.1
where the time goes:
time: 533 us
  waiting for transfers between devices  329 us (62%)
  blocking collectives  74.8 us (14%)
  matrix products  42.3 us (8%)
  other arithmetic  40.9 us (8%)
  local copies, waits for them, and re-layouts  19.9 us (4%)
  between operations  14 us (3%)
  starting transfers between devices  11.6 us (2%)
    psum x1, waiting for transfers between devices, on_device(): trunk_grad = lax.psum(trunk_local, ('dp', 'expert'))  250 us
    all_to_all x1, waiting for transfers between devices, on_device(): lax.all_to_all(predicted.reshape(experts, capacity, width), 'expert', spl...  51.1 us
    all_to_all x1, blocking collectives, on_device(): lax.all_to_all(pack(trunk_out), 'expert', split_axis=0, concat_axis=0, ti...  40.8 us
    all_to_all x1, blocking collectives, on_device(): lax.all_to_all(pack(row_error), 'expert', split_axis=0, concat_axis=0, ti...  34 us
    all_to_all x1, waiting for transfers between devices, on_device(): lax.all_to_all(input_grad.reshape(experts, capacity, width), 'expert', sp...  28 us
    another operation x3, other arithmetic  18.2 us
    scatter x2, other arithmetic, pack(): empty.at[places].set(values).reshape((experts, capacity) + values.shape[1:])  11.7 us
  transfers between devices with their start and end apart: 5, of which 3 were waited for; matrix products, arithmetic and copies ran while one was open for 9% of the time, Pallas kernels for 0%

commit v1 on v0

--- a/solution.py
+++ b/solution.py
@@ -117,7 +117,8 @@
     trunk_local = lax.dot_general(
         features, trunk_slope, (((0,), (0,)), ((), ())), preferred_element_type=jnp.float32
     )
-    trunk_grad = lax.psum(trunk_local, ("dp", "expert"))
+    blocks = lax.all_gather(trunk_local, ("dp", "expert"), axis=0, tiled=False)
+    trunk_grad = blocks.sum(axis=0)
     grads = jnp.stack([grad_up, grad_down])[None]
     grad_shard = lax.psum_scatter(grads, "dp", scatter_dimension=3, tiled=True)
     new_params, new_first, new_second = adam_update(

time: 533 us -> 515 us (0.966)
  waiting for transfers between devices: 329 us -> 261 us
  blocking collectives: 74.8 us -> 109 us
  other arithmetic: 40.9 us -> 62.7 us
  starting transfers between devices: 11.6 us -> 6.09 us
    psum x1 -> x0, waiting for transfers between devices: 250 us -> none  [on_device(): trunk_grad = lax.psum(trunk_local, ('dp', 'expert'))]
    all_gather x0 -> x1, waiting for transfers between devices: none -> 210 us  [on_device(): blocks = lax.all_gather(trunk_local, ('dp', 'expert'), axis=0, tiled=False)]
    all_to_all x0 -> x1, blocking collectives: none -> 34.4 us  [on_device(): lax.all_to_all(input_grad.reshape(experts, capacity, width), 'expert', sp...]
    all_to_all x1 -> x0, waiting for transfers between devices: 28 us -> none  [on_device(): lax.all_to_all(input_grad.reshape(experts, capacity, width), 'expert', sp...]
    reduce_sum x0 -> x1, other arithmetic: none -> 21.8 us  [on_device(): trunk_grad = blocks.sum(axis=0)]
    all_to_all x1 -> x0, starting transfers between devices: 5.69 us -> none  [on_device(): lax.all_to_all(input_grad.reshape(experts, capacity, width), 'expert', sp...]
  transfers between devices with their start and end apart: 5 -> 4, of which waited for: 3 -> 2; matrix products, arithmetic and copies ran while one was open for 9% -> 10% of each run, Pallas kernels for 0% -> 0%
where the time goes in v1:
time: 515 us; the launch traced here: 514 us
  waiting for transfers between devices  261 us (51%)
  blocking collectives  109 us (21%)
  other arithmetic  62.7 us (12%)
  matrix products  41.5 us (8%)
  local copies, waits for them, and re-layouts  19.3 us (4%)
  between operations  14.1 us (3%)
  starting transfers between devices  6.09 us (1%)
    all_gather x1, waiting for transfers between devices, on_device(): blocks = lax.all_gather(trunk_local, ('dp', 'expert'), axis=0, tiled=False)  210 us
    all_to_all x1, waiting for transfers between devices, on_device(): lax.all_to_all(predicted.reshape(experts, capacity, width), 'expert', spl...  51.1 us
    all_to_all x1, blocking collectives, on_device(): lax.all_to_all(pack(trunk_out), 'expert', split_axis=0, concat_axis=0, ti...  40.8 us
    all_to_all x1, blocking collectives, on_device(): lax.all_to_all(input_grad.reshape(experts, capacity, width), 'expert', sp...  34.4 us
    all_to_all x1, blocking collectives, on_device(): lax.all_to_all(pack(row_error), 'expert', split_axis=0, concat_axis=0, ti...  34 us
    reduce_sum x1, other arithmetic, on_device(): trunk_grad = blocks.sum(axis=0)  21.8 us
    another operation x3, other arithmetic  18.2 us
    scatter x2, other arithmetic, pack(): empty.at[places].set(values).reshape((experts, capacity) + values.shape[1:])  11.9 us
  transfers between devices with their start and end apart: 4, of which 2 were waited for; matrix products, arithmetic and copies ran while one was open for 10% of the time, Pallas kernels for 0%

profile of v1, /device:TPU:2, one launch (start us, length us, event | category | flops | bytes accessed | tf_op | source)
XLA Modules:
  0.0 513.6 jit_solution(2242039293671178522)
XLA Ops:
  7.2 0.0 copy-start
  7.2 0.0 copy-start.14
  7.2 0.0 copy-start.15
  7.2 0.0 all-gather.4.cloned.1.call-start
  7.3 2.2 convert_element_type.38
  9.4 0.0 all-gather.4.cloned.1.call-update
  9.5 0.7 fusion.15
  10.2 18.0 %reduce-window.6 = s32[64,8,128]{2,1,0:T(8,128)S(1)} reduce-window(s32[64,8,128]{2,1,0:T(8,128)S(1)} %fusion.15, s32[]{:T(128)} %constant.18.clone.1), window={size=1x1x128 pad=0_0x0_0x127_0}, to_apply=%region_0.1 | reduce-window | flops 8323072 | bytes 524292 | tf_op jit(solution)/shard_map/reduce-window
  28.2 0.1 slice.22
  28.3 0.1 copy.13
  28.5 0.1 copy.14
  28.6 0.1 broadcast_add_fusion
  28.7 0.7 fusion.16
  29.4 3.9 gather_fusion
  33.4 0.1 fusion.14
  33.5 0.4 fusion.18
  33.9 0.0 copy-start.11
  33.9 6.0 %scatter_custom_fusion = bf16[2048,256]{1,0:T(8,128)(2,1)S(1)} fusion(s32[1024]{0:T(1024)S(1)} %bitcast.71, bf16[]{:T(256)} %constant.22.clone.1, f32[1024,256]{1,0:T(8,128)S(1)} %fusion.18, f32[]{:T(128)} %constant.15.clone.1, bf16[1024,256]{1,0:T(8,128)(2,1)S(1)} %gather_fusion, pred[1024]{0:T(1024)(128)(4,1)S(1)} %compare_and_fusion), kind=kCustom, calls=%fused_computation.32 | custom fusion | flops 2097152 | bytes 2622470 | tf_op jit(solution)/shard_map/scatter | solution.py:85
  39.9 40.8 %all_to_all.20 = bf16[64,32,256]{2,1,0:T(8,128)(2,1)S(1)} all-to-all(bf16[64,32,256]{2,1,0:T(8,128)(2,1)S(1)} %bitcast.65), channel_id=1, replica_groups=mesh['dp'=4,'expert'=64] {'expert'}, dimensions={0} | all-to-all | bytes 2097152 | tf_op jit(solution)/shard_map/all_to_all | solution.py:90
  80.7 9.8 %multiply_convert_fusion.1 = (bf16[2048,2048]{1,0:T(8,128)(2,1)S(1)}, f32[2048,2048]{1,0:T(8,128)}) fusion(bf16[2048,256]{1,0:T(8,128)(2,1)S(1)} %bitcast.60, bf16[1,2,256,2048]{3,2,1,0:T(8,128)(2,1)} %all-gather.4.cloned.1.call-done), kind=kOutput, calls=%fused_computation.6 | convolution fusion | flops 2168455168 | bytes 27262976 | tf_op jit(solution)/shard_map/dot_general | solution.py:20
  90.5 3.2 copy-done.2
  93.7 3.8 fusion.1
  97.5 5.6 %all-to-all-start.1 = ((f32[64,32,256]{2,1,0:T(8,128)}), f32[64,32,256]{2,1,0:T(8,128)S(1)}, u32[]{:S(2)}, u32[]{:S(2)}) async-start(f32[64,32,256]{2,1,0:T(8,128)} %fusion.1), calls=%async_computation.1 | async-start | bytes 4194304 | tf_op jit(solution)/shard_map/all_to_all | solution.py:94
  103.1 0.2 reduce-scatter.2.cloned.1.call-start
  103.4 51.1 %all-to-all-done.1 = f32[64,32,256]{2,1,0:T(8,128)S(1)} async-done(((f32[64,32,256]{2,1,0:T(8,128)}), f32[64,32,256]{2,1,0:T(8,128)S(1)}, u32[]{:S(2)}, u32[]{:S(2)}) %all-to-all-start.1) | async-done | bytes 2097184 | tf_op jit(solution)/shard_map/all_to_all | solution.py:94
  154.5 3.5 gather_fusion.1
  157.9 0.0 copy-start.4
  158.0 5.9 %scatter_custom_fusion.1 = bf16[2048,256]{1,0:T(8,128)(2,1)S(1)} fusion(s32[1024]{0:T(1024)S(1)} %bitcast.73, f32[1024,256]{1,0:T(8,128)S(1)} %gather_fusion.1, bf16[1024,256]{1,0:T(8,128)(2,1)} %param.11, f32[]{:T(128)} %constant.16.clone.1, bf16[]{:T(256)} %constant.22.clone.1), kind=kCustom, calls=%fused_computation.29 | custom fusion | flops 1048576 | bytes 2621446 | tf_op jit(solution)/shard_map/scatter | solution.py:85
  163.9 34.0 %all_to_all.21 = bf16[64,32,256]{2,1,0:T(8,128)(2,1)S(1)} all-to-all(bf16[64,32,256]{2,1,0:T(8,128)(2,1)S(1)} %bitcast.64), channel_id=1, replica_groups=mesh['dp'=4,'expert'=64] {'expert'}, dimensions={0} | all-to-all | bytes 2097152 | tf_op jit(solution)/shard_map/all_to_all | solution.py:102
  197.9 5.9 %convolution_bitcast_fusion = f32[1,256,2048]{2,1,0:T(8,128)S(1)} fusion(bf16[2048,256]{1,0:T(8,128)(2,1)S(1)} %bitcast.62, bf16[2048,2048]{1,0:T(8,128)(2,1)} %copy-done.2), kind=kOutput, calls=%fused_computation.9 | convolution fusion | flops 2147483648 | bytes 11534336 | tf_op jit(solution)/shard_map/dot_general | solution.py:29
  203.8 0.0 copy-start.7
  203.9 10.4 %multiply_convert_fusion = bf16[2048,2048]{1,0:T(8,128)(2,1)S(1)} fusion(f32[2048,2048]{1,0:T(8,128)} %get-tuple-element.9, bf16[2048,256]{1,0:T(8,128)(2,1)S(1)} %bitcast.63, bf16[1,2,256,2048]{3,2,1,0:T(8,128)(2,1)S(1)} %copy-done.17), kind=kOutput, calls=%fused_computation.5 | convolution fusion | flops 2185232384 | bytes 27262976 | tf_op jit(solution)/shard_map/dot_general | solution.py:32
  214.2 3.2 copy-done.3
  217.5 2.4 convolution_bitcast_fusion.1
  219.8 2.3 maximum_bitcast_fusion
  222.1 0.0 reduce-scatter.2.cloned.1.call-update
  222.1 0.3 all-gather.6.cloned.1.call-start
  222.4 6.0 %convolution_convert_fusion = bf16[2048,256]{1,0:T(8,128)(2,1)S(1)} fusion(bf16[2048,2048]{1,0:T(8,128)(2,1)} %copy-done.3, bf16[1,2,256,2048]{3,2,1,0:T(8,128)(2,1)} %all-gather.4.cloned.1.call-done), kind=kOutput, calls=%fused_computation.11 | convolution fusion | flops 2148007936 | bytes 10485760 | tf_op jit(solution)/shard_map/dot_general | solution.py:37
  228.4 0.0 copy-start.5
  228.4 34.4 %all_to_all.22 = bf16[64,32,256]{2,1,0:T(8,128)(2,1)S(1)} all-to-all(bf16[64,32,256]{2,1,0:T(8,128)(2,1)S(1)} %bitcast.66), channel_id=1, replica_groups=mesh['dp'=4,'expert'=64] {'expert'}, dimensions={0} | all-to-all | bytes 2097152 | tf_op jit(solution)/shard_map/all_to_all | solution.py:108
  262.8 5.0 gather_fusion.2
  267.8 2.9 fusion.12
  270.7 0.0 all-gather.6.cloned.1.call-update
  270.7 0.2 multiply_reduce_fusion
  271.0 0.6 broadcast_multiply_fusion
  271.6 4.0 divide_subtract_fusion
  275.6 209.7 %all-gather.6.cloned.1.call-done = f32[65536,256]{1,0:T(8,128)} async-done(((f32[256,256]{1,0:T(8,128)}), f32[65536,256]{1,0:T(8,128)}) %all-gather.6.cloned.1.call-update) | async-done | bytes 67108880 | tf_op jit(solution)/shard_map/all_gather | solution.py:120
  485.2 21.8 %reduce_sum.28 = f32[256,256]{1,0:T(8,128)} reduce(f32[256,256,256]{2,1,0:T(8,128)} %bitcast.17, f32[]{:T(128)} %constant.17.clone.1), dimensions={0}, to_apply=%region_5.6 | reduce | flops 16711680 | bytes 67371008 | tf_op jit(solution)/shard_map/reduce_sum | solution.py:121
  (35 shorter events, 0.1 us)
Async XLA Ops:
  7.2 22.3 %copy-start = (bf16[2048,256]{1,0:T(8,128)(2,1)S(1)}, bf16[2048,256]{1,0:T(8,128)(2,1)}, u32[]{:S(2)}) copy-start(bf16[2048,256]{1,0:T(8,128)(2,1)} %param.8) | copy-start | bytes 3145732
  7.2 26.2 %copy-start.14 = (s32[1024,1]{0,1:T(1,128)S(1)}, s32[1024,1]{0,1:T(1,128)}, u32[]{:S(2)}) copy-start(s32[1024,1]{0,1:T(1,128)} %param.10) | copy-start | bytes 12292
  7.2 26.3 %copy-start.15 = (s32[1024]{0:T(1024)S(1)}, s32[1024]{0:T(1024)}, u32[]{:S(2)}) copy-start(s32[1024]{0:T(1024)} %param.9) | copy-start | bytes 12292
  7.2 26.3 %copy-start.13 = (bf16[256,256]{1,0:T(8,128)(2,1)S(1)}, bf16[256,256]{1,0:T(8,128)(2,1)}, u32[]{:S(2)}) copy-start(bf16[256,256]{1,0:T(8,128)(2,1)} %param.12) | copy-start | bytes 393220
  7.2 73.5 %all-gather.4.cloned.1.call-start = ((), (), s32[]{:S(2)}) async-start(), calls=%async_computation.5 | async-start | bytes 2621440 | tf_op jit(solution)/shard_map/all_gather | solution.py:87
  33.4 57.1 %copy-start.8 = (bf16[1024,256]{1,0:T(8,128)(2,1)}, bf16[1024,256]{1,0:T(8,128)(2,1)S(1)}, u32[]{:S(2)}) copy-start(bf16[1024,256]{1,0:T(8,128)(2,1)S(1)} %gather_fusion) | copy-start | bytes 1572868
  33.9 6.0 %copy-start.11 = (f32[1024,256]{1,0:T(8,128)}, f32[1024,256]{1,0:T(8,128)S(1)}, u32[]{:S(2)}) copy-start(f32[1024,256]{1,0:T(8,128)S(1)} %fusion.18) | copy-start | bytes 3145732
  80.7 9.8 %copy-start.6 = (bf16[64,32,256]{2,1,0:T(8,128)(2,1)}, bf16[64,32,256]{2,1,0:T(8,128)(2,1)S(1)}, u32[]{:S(2)}) copy-start(bf16[64,32,256]{2,1,0:T(8,128)(2,1)S(1)} %all_to_all.20) | copy-start | bytes 3145732
  80.7 13.0 %copy-start.16 = (bf16[1,2,256,2048]{3,2,1,0:T(8,128)(2,1)S(1)}, bf16[1,2,256,2048]{3,2,1,0:T(8,128)(2,1)}, u32[]{:S(2)}) copy-start(bf16[1,2,256,2048]{3,2,1,0:T(8,128)(2,1)} %all-gather.4.cloned.1.call-done) | copy-start | bytes 6291460
  90.5 3.2 copy-start.2
  97.5 56.9 %all-to-all-start.1 = ((f32[64,32,256]{2,1,0:T(8,128)}), f32[64,32,256]{2,1,0:T(8,128)S(1)}, u32[]{:S(2)}, u32[]{:S(2)}) async-start(f32[64,32,256]{2,1,0:T(8,128)} %fusion.1), calls=%async_computation.1 | async-start | bytes 4194304 | tf_op jit(solution)/shard_map/all_to_all | solution.py:94
  103.1 168.4 %reduce-scatter.2.cloned.1.call-start = ((), (), s32[]{:S(2)}) async-start(), calls=%async_computation.6 | async-start | bytes 5242880 | tf_op jit(solution)/shard_map/reduce_scatter | solution.py:123
  157.9 45.9 %copy-start.4 = (f32[1024,256]{1,0:T(8,128)}, f32[1024,256]{1,0:T(8,128)S(1)}, u32[]{:S(2)}) copy-start(f32[1024,256]{1,0:T(8,128)S(1)} %gather_fusion.1) | copy-start | bytes 3145732
  197.9 5.9 %copy-start.17 = (bf16[1,2,256,2048]{3,2,1,0:T(8,128)(2,1)S(1)}, bf16[1,2,256,2048]{3,2,1,0:T(8,128)(2,1)}, u32[]{:S(2)}) copy-start(bf16[1,2,256,2048]{3,2,1,0:T(8,128)(2,1)} %all-gather.4.cloned.1.call-done) | copy-start | bytes 6291460
  203.8 13.6 %copy-start.7 = (bf16[64,32,256]{2,1,0:T(8,128)(2,1)S(1)}, bf16[64,32,256]{2,1,0:T(8,128)(2,1)}, u32[]{:S(2)}) copy-start(bf16[64,32,256]{2,1,0:T(8,128)(2,1)} %copy-done.6) | copy-start | bytes 3145732
  214.2 3.2 copy-start.3
  222.1 45.7 %copy-start.9 = (bf16[1024,256]{1,0:T(8,128)(2,1)S(1)}, bf16[1024,256]{1,0:T(8,128)(2,1)}, u32[]{:S(2)}) copy-start(bf16[1024,256]{1,0:T(8,128)(2,1)} %copy-done.8) | copy-start | bytes 1572868
  222.1 263.1 %all-gather.6.cloned.1.call-start = ((), (), s32[]{:S(2)}) async-start(), calls=%async_computation.7 | async-start | bytes 67371008 | tf_op jit(solution)/shard_map/all_gather | solution.py:120
  228.4 42.3 %copy-start.5 = (f32[1024,256]{1,0:T(8,128)S(1)}, f32[1024,256]{1,0:T(8,128)}, u32[]{:S(2)}) copy-start(f32[1024,256]{1,0:T(8,128)} %copy-done.4) | copy-start | bytes 3145732
  228.4 42.3 %copy-start.12 = (bf16[1024,256]{1,0:T(8,128)(2,1)S(1)}, bf16[1024,256]{1,0:T(8,128)(2,1)}, u32[]{:S(2)}) copy-start(bf16[1024,256]{1,0:T(8,128)(2,1)} %param.11) | copy-start | bytes 1572868
  267.8 3.8 copy-start.10
  485.2 21.8 %copy-start.1 = (bf16[2048,256]{1,0:T(8,128)(2,1)S(1)}, bf16[2048,256]{1,0:T(8,128)(2,1)}, u32[]{:S(2)}) copy-start(bf16[2048,256]{1,0:T(8,128)(2,1)} %param.8) | copy-start | bytes 3145732
Sparse Core Ops, SparseCore 0:
  10.4 35.3 all-gather.3
  222.2 44.4 reduce-scatter.1
  271.7 213.4 all-gather.5
